TPU v7x, 32 devices: a whole 2x2x4 slice. The times are simulated.
32 devices in a mesh: group: 4 (over y, core), inner: 8 (over z, x).
Axes of the slice: x: 2, y: 2, z: 4, core: 2. Of those that a mesh axis runs over, the one named last changes fastest.
Arguments:
- grad_out: bfloat16 [4096, 2048], P(('group', 'inner')), may hold values from -4 to 4
- hidden_in: bfloat16 [4096, 2048], P(('group', 'inner')), may hold values from -6 to 6
- norm_gain: float32 [2048], replicated, may hold values from 0.5 to 1.5
- expert_ids: int32 [4096, 8], P(('group', 'inner')), may hold values from 0 to 31, all different within a row; in each aligned block of 128 rows (0 to 127, 128 to 255, ...) at most 40 rows name the same one
- gate_weights: float32 [4096, 8], P(('group', 'inner')), may hold values from 0.02 to 0.5
- gate_proj: bfloat16 [32, 2048, 768], P(('group', 'inner')), may hold values from -0.125 to 0.125
- up_proj: bfloat16 [32, 2048, 768], P(('group', 'inner')), may hold values from -0.125 to 0.125
- down_proj: bfloat16 [32, 768, 2048], P(('group', 'inner')), may hold values from -0.21875 to 0.21875
- out_proj: bfloat16 [4096, 2048], P('inner'), may hold values from -0.09375 to 0.09375
- query_rows: bfloat16 [4096, 4096], P('group', 'inner'), may hold values from -140 to 140
- key_rows: bfloat16 [4096, 4096], P('group', 'inner'), may hold values from -7 to 7
- value_rows: bfloat16 [4096, 4096], P('group', 'inner'), may hold values from -6 to 6
Outputs:
- grad_hidden: bfloat16 [4096, 2048], P(('group', 'inner'))
- grad_gate: bfloat16 [4096, 8], P(('group', 'inner'))
- grad_queries: bfloat16 [4096, 4096], P('group', 'inner')
- grad_keys: bfloat16 [4096, 4096], P('group', 'inner')
- grad_values: bfloat16 [4096, 4096], P('group', 'inner')
Inputs may be any that keep to these rules, and one draw needn't show every extreme that they name: `expert_ids`: each row names 8 different experts; in the rows of one device no expert is named more than 40 times, a bound that some block reaches.
All inputs are finite; a program needn't handle non-finite values.
Results may differ from a plain program's by a relative error of at most 0.019.
Values may be sent and summed in bfloat16 or wider, within the bound.
A program may use at most 128 MiB of HBM per device.

v0:
```python
import jax
import jax.numpy as jnp
from jax import lax
from jax.sharding import PartitionSpec as P

HD = 128
SEQS = 2


def dot_rt(left, right):
    return lax.dot_general(
        left, right, (((1,), (1,)), ((), ())), preferred_element_type=jnp.float32
    )


def dot_lt(left, right):
    return lax.dot_general(
        left, right, (((0,), (0,)), ((), ())), preferred_element_type=jnp.float32
    )


def expert_backward(arrived, gate_mat, up_mat, down_mat):
    model_width = gate_mat.shape[0]
    grad_in = arrived[:, :model_width]
    normed_in = arrived[:, model_width:]
    gate_pre = jnp.dot(normed_in, gate_mat, preferred_element_type=jnp.float32)
    up_pre = jnp.dot(normed_in, up_mat, preferred_element_type=jnp.float32)
    sigma = jax.nn.sigmoid(gate_pre)
    act = gate_pre * sigma
    slope = sigma * (1.0 + gate_pre * (1.0 - sigma))
    expert_hidden = act * up_pre
    grad_hid = dot_rt(grad_in, down_mat)
    gate_score = jnp.sum(grad_hid * expert_hidden, axis=1).astype(jnp.bfloat16)
    grad_gatepre = (grad_hid * up_pre * slope).astype(jnp.bfloat16)
    grad_uppre = (grad_hid * act).astype(jnp.bfloat16)
    pair_grad = (dot_rt(grad_gatepre, gate_mat) + dot_rt(grad_uppre, up_mat)).astype(jnp.bfloat16)
    return (pair_grad, gate_score)


def local(
    grad_out,
    hidden_in,
    norm_gain,
    expert_ids,
    gate_weights,
    gate_proj,
    up_proj,
    down_proj,
    out_proj,
    query_rows,
    key_rows,
    value_rows,
):
    tok_dev, model_width = grad_out.shape
    top_count = expert_ids.shape[1]
    groups = lax.axis_size("group")
    inner_size = lax.axis_size("inner")
    experts = groups * inner_size
    capacity = max(2, 5 * tok_dev * top_count // (4 * experts))
    local_heads = out_proj.shape[0] // HD
    length = query_rows.shape[0] // SEQS
    att_scale = HD ** (-0.5)
    causal = jnp.arange(length)[:, None] >= jnp.arange(length)[None, :]

    def by_head(matrix):
        return (
            matrix.reshape(SEQS, length, local_heads, HD)
            .transpose(0, 2, 1, 3)
            .reshape(SEQS * local_heads, length, HD)
        )

    def by_token(stacked):
        return (
            stacked.reshape(SEQS, local_heads, length, HD)
            .transpose(0, 2, 1, 3)
            .reshape(SEQS * length, local_heads * HD)
        )

    def masked_scores(query, key_part):
        return jnp.where(causal, dot_rt(query, key_part) * att_scale, -jnp.inf)

    query_items = by_head(query_rows)
    key_items = by_head(key_rows)
    value_items = by_head(value_rows)
    hid_full = hidden_in.astype(jnp.float32)
    inv_rms = lax.rsqrt(jnp.mean(hid_full * hid_full, axis=1, keepdims=True) + 1e-06)
    normal_rows = hid_full * inv_rms
    normed = (normal_rows * norm_gain).astype(jnp.bfloat16)
    flat_ids = expert_ids.reshape(-1)
    pair_count = flat_ids.shape[0]
    onehot = (flat_ids[:, None] == jnp.arange(experts, dtype=jnp.int32)[None, :]).astype(jnp.int32)
    earlier = jnp.cumsum(onehot, axis=0) - onehot
    slot_index = jnp.sum(earlier * onehot, axis=1)
    target = flat_ids * capacity + slot_index
    token_rows = jnp.concatenate([grad_out, normed], axis=1)
    blank_row = jnp.zeros((1, 2 * model_width), jnp.bfloat16)
    owner_token = (
        jnp.full((experts * capacity,), tok_dev, jnp.int32)
        .at[target]
        .set(jnp.arange(pair_count, dtype=jnp.int32) // top_count)
    )
    send_rows = jnp.concatenate([token_rows, blank_row], axis=0)
    outgoing = send_rows[owner_token]
    arrived = lax.all_to_all(
        outgoing.reshape(experts, capacity, 2 * model_width),
        ("group", "inner"),
        split_axis=0,
        concat_axis=0,
        tiled=True,
    )
    arrived = arrived.reshape(experts * capacity, 2 * model_width)
    pair_grad, gate_score = expert_backward(arrived, gate_proj[0], up_proj[0], down_proj[0])
    returned, score_back = (
        lax.all_to_all(
            pair_grad.reshape(experts, capacity, model_width),
            ("group", "inner"),
            split_axis=0,
            concat_axis=0,
            tiled=True,
        ),
        lax.all_to_all(
            gate_score.reshape(experts, capacity),
            ("group", "inner"),
            split_axis=0,
            concat_axis=0,
            tiled=True,
        ),
    )
    returned = returned.reshape(experts * capacity, model_width)[target]
    grad_gate = score_back.reshape(experts * capacity)[target].reshape(tok_dev, top_count)
    moe_grad = jnp.einsum(
        "tk,tkd->td",
        gate_weights,
        returned.reshape(tok_dev, top_count, model_width).astype(jnp.float32),
    )
    scaled = moe_grad * norm_gain
    inner_mean = jnp.mean(scaled * normal_rows, axis=1, keepdims=True)
    grad_hidden = (
        grad_out.astype(jnp.float32) + inv_rms * (scaled - normal_rows * inner_mean)
    ).astype(jnp.bfloat16)
    grad_attn = dot_rt(lax.all_gather(grad_hidden, "inner", axis=0, tiled=True), out_proj).astype(
        jnp.bfloat16
    )
    grad_items = by_head(grad_attn)

    def attend(block_item):
        query, key_part, value, grad_part = block_item
        scores = masked_scores(query, key_part)
        peak = jnp.max(scores, axis=1, keepdims=True)
        exp_scores = jnp.exp(scores - peak)
        probs = exp_scores / jnp.sum(exp_scores, axis=1, keepdims=True)
        probs_half = probs.astype(jnp.bfloat16)
        grad_v = dot_lt(probs_half, grad_part).astype(jnp.bfloat16)
        grad_probs = dot_rt(grad_part, value)
        delta = jnp.sum(probs * grad_probs, axis=1, keepdims=True)
        grad_scores = (probs * (grad_probs - delta)).astype(jnp.bfloat16)
        grad_q = (
            att_scale * jnp.dot(grad_scores, key_part, preferred_element_type=jnp.float32)
        ).astype(jnp.bfloat16)
        grad_k = (att_scale * dot_lt(grad_scores, query)).astype(jnp.bfloat16)
        return (grad_q, grad_k, grad_v)

    results = lax.map(
        lambda block_item: attend(block_item), (query_items, key_items, value_items, grad_items)
    )
    return (
        grad_hidden,
        grad_gate,
        by_token(results[0]),
        by_token(results[1]),
        by_token(results[2]),
    )


def solution(mesh):
    in_specs = (
        P(("group", "inner"), None),
        P(("group", "inner"), None),
        P(),
        P(("group", "inner"), None),
        P(("group", "inner"), None),
        P(("group", "inner"), None, None),
        P(("group", "inner"), None, None),
        P(("group", "inner"), None, None),
        P("inner", None),
        P("group", "inner"),
        P("group", "inner"),
        P("group", "inner"),
    )
    out_specs = (
        P(("group", "inner"), None),
        P(("group", "inner"), None),
        P("group", "inner"),
        P("group", "inner"),
        P("group", "inner"),
    )
    return jax.shard_map(local, mesh=mesh, in_specs=in_specs, out_specs=out_specs, check_vma=False)
```

profile of v0, /device:TPU:0, one launch (start us, length us, event | category | flops | bytes accessed | tf_op | source)
XLA Modules:
  0.0 628.6 jit_solution(9642393507748024651)
XLA Ops:
  9.0 9.0 %reduce-window.6 = s32[32,8,128]{2,1,0:T(8,128)S(1)} reduce-window(s32[32,8,128]{2,1,0:T(8,128)S(1)} %fusion.68, s32[]{:T(128)} %copy.83), window={size=1x1x128 pad=0_0x0_0x127_0}, to_apply=%region_1.0 | reduce-window | flops 4161536 | bytes 262148 | tf_op jit(solution)/shard_map/reduce-window
  18.7 4.3 scatter_custom_fusion
  25.6 2.2 fusion.56
  27.8 20.2 %gather_fusion = bf16[1280,4096]{1,0:T(8,128)(2,1)} fusion(bf16[129,4096]{1,0:T(8,128)(2,1)} %fusion.56, s32[2048]{0:T(1024)S(1)} %pad_clamp_fusion), kind=kCustom, calls=%fused_computation | custom fusion | bytes 20976640 | tf_op jit(solution)/shard_map/gather | solution.py:103
  47.9 237.0 %all_to_all.16 = bf16[32,40,4096]{2,1,0:T(8,128)(2,1)S(1)} all-to-all(bf16[32,40,4096]{2,1,0:T(8,128)(2,1)} %bitcast.146), channel_id=1, replica_groups=mesh['group'=4,'inner'=8] {'group','inner'}, dimensions={0} | all-to-all | bytes 20971520 | tf_op jit(solution)/shard_map/all_to_all | solution.py:104
  285.0 4.7 fusion.37
  289.7 6.4 %fusion.39 = f32[1280,768]{0,1:T(8,128)} fusion(bf16[1280,4096]{1,0:T(8,128)(2,1)S(1)} %bitcast.148, bf16[1,2048,768]{2,1,0:T(8,128)(2,1)S(1)} %copy-done.9), kind=kOutput, calls=%fused_computation.50 | convolution fusion | flops 4026531840 | bytes 12320768 | tf_op jit(solution)/shard_map/dot_general | solution.py:27
  296.1 7.7 %multiply_reduce_fusion.1 = (bf16[1280]{0:T(1024)(128)(2,1)S(1)}, f32[1280,768]{0,1:T(8,128)}) fusion(f32[1280,768]{0,1:T(8,128)} %fusion.39, f32[1280,768]{0,1:T(8,128)S(1)} %fusion.37, bf16[1,768,2048]{2,1,0:T(8,128)(2,1)S(1)} %copy-done.8, bf16[1280,4096]{1,0:T(8,128)(2,1)S(1)} %bitcast.149), kind=kOutput, calls=%fused_computation.54 | convolution fusion | flops 4033411840 | bytes 20187648 | tf_op jit(solution)/shard_map/dot_general | solution.py:11
  303.8 12.5 %fusion.44 = f32[1280,2048]{1,0:T(8,128)} fusion(bf16[1,2048,768]{2,1,0:T(8,128)(2,1)S(1)} %copy-done, f32[1280,768]{0,1:T(8,128)S(1)} %fusion.37, f32[1280,768]{0,1:T(8,128)} %get-tuple-element.106, f32[1280,768]{0,1:T(8,128)} %fusion.39), kind=kOutput, calls=%fused_computation.59 | convolution fusion | flops 4036362240 | bytes 25427968 | tf_op jit(solution)/shard_map/dot_general | solution.py:11
  316.3 10.3 %add_convert_fusion = bf16[1280,2048]{1,0:T(8,128)(2,1)} fusion(f32[1280,2048]{1,0:T(8,128)} %fusion.44, bf16[1,2048,768]{2,1,0:T(8,128)(2,1)S(1)} %copy-done.9, f32[1280,768]{0,1:T(8,128)} %get-tuple-element.106, f32[1280,768]{0,1:T(8,128)S(1)} %fusion.37), kind=kOutput, calls=%fused_computation.45 | convolution fusion | flops 4037672960 | bytes 26738688 | tf_op jit(solution)/shard_map/dot_general | solution.py:11
  326.7 3.7 all-to-all-start.1
  330.6 117.3 %all-to-all-done.1 = bf16[32,40,2048]{2,1,0:T(8,128)(2,1)} async-done(((bf16[32,40,2048]{2,1,0:T(8,128)(2,1)}), bf16[32,40,2048]{2,1,0:T(8,128)(2,1)}, u32[]{:S(2)}, u32[]{:S(2)}) %all-to-all-start.1) | async-done | bytes 5242912 | tf_op jit(solution)/shard_map/all_to_all | solution.py:114
  447.9 12.0 %gather_fusion.1 = bf16[1024,2048]{1,0:T(8,128)(2,1)} fusion(bf16[1280,2048]{1,0:T(8,128)(2,1)} %bitcast.10, s32[1024]{0:T(1024)S(1)} %broadcast_clamp_fusion), kind=kCustom, calls=%fused_computation.1 | custom fusion | bytes 8392704 | tf_op jit(solution)/shard_map/gather | solution.py:129
  460.0 3.6 fusion.41
  466.2 2.8 all-to-all-start.2
  476.0 6.8 %gather_fusion.2 = bf16[1024]{0:T(1024)(128)(2,1)S(1)} fusion(bf16[1280]{0:T(1024)(128)(2,1)S(1)} %reshape.157, s32[1024]{0:T(1024)S(1)} %broadcast_clamp_fusion), kind=kCustom, calls=%fused_computation.2 | custom fusion | bytes 8192 | tf_op jit(solution)/shard_map/gather | solution.py:130
  483.6 52.7 %all-gather.2.cloned.1.call-done = bf16[1024,2048]{1,0:T(8,128)(2,1)} async-done(((bf16[128,2048]{1,0:T(8,128)(2,1)}), bf16[1024,2048]{1,0:T(8,128)(2,1)}) %all-gather.2.cloned.1.call-update) | async-done | bytes 4194320 | tf_op jit(solution)/shard_map/all_gather | solution.py:141
  536.3 5.2 convolution_convert_fusion.1
  542.9 69.7 %while.15 = (s32[]{:T(128)}, bf16[8,512,128]{2,1,0:T(8,128)(2,1)}, bf16[8,512,128]{2,1,0:T(8,128)(2,1)}, bf16[8,512,128]{2,1,0:T(8,128)(2,1)}, bf16[8,512,128]{2...) while((s32[]{:T(128)}, bf16[8,512,128]{2,1,0:T(8,128)(2,1)}, ...), condition=%wide.region_11.12_spmd.clone, body=%wide.region_7.11_spmd.clone.sunk | while | flops 340589056 | bytes 10251357 | solution.py:163
  544.4 1.9 fusion.103
  549.7 1.9 fusion.101
  558.4 1.9 fusion.101
  567.1 1.9 fusion.101
  570.5 1.9 fusion.103
  575.8 1.9 fusion.101
  584.6 1.9 fusion.101
  593.3 1.9 fusion.101
  602.0 1.9 fusion.101
  610.7 1.9 fusion.101
  612.6 2.0 copy.48
  614.6 2.0 copy.49
  616.7 2.2 copy.47
  (113 shorter events, 70.3 us)
Async XLA Ops:
  7.2 277.8 %copy-start = (bf16[1,2048,768]{2,1,0:T(8,128)(2,1)S(1)}, bf16[1,2048,768]{2,1,0:T(8,128)(2,1)}, u32[]{:S(2)}) copy-start(bf16[1,2048,768]{2,1,0:T(8,128)(2,1)} %param.19) | copy-start | bytes 9437188
  285.0 4.7 copy-start.9
  289.7 6.4 %copy-start.8 = (bf16[1,768,2048]{2,1,0:T(8,128)(2,1)S(1)}, bf16[1,768,2048]{2,1,0:T(8,128)(2,1)}, u32[]{:S(2)}) copy-start(bf16[1,768,2048]{2,1,0:T(8,128)(2,1)} %param.21) | copy-start | bytes 9437188
  326.7 3.8 copy-start.7
  326.7 121.2 %all-to-all-start.1 = ((bf16[32,40,2048]{2,1,0:T(8,128)(2,1)}), bf16[32,40,2048]{2,1,0:T(8,128)(2,1)}, u32[]{:S(2)}, u32[]{:S(2)}) async-start(bf16[32,40,2048]{2,1,0:T(8,128)(2,1)} %bitcast.150), calls=%async_computation.1 | async-start | bytes 10485760 | tf_op jit(solution)/shard_map/all_to_all | solution.py:114
  330.4 205.9 %all-gather.2.cloned.1.call-start = ((), (), s32[]{:S(2)}) async-start(), calls=%async_computation.3 | async-start | bytes 4718592 | tf_op jit(solution)/shard_map/all_gather | solution.py:141
  460.0 3.6 copy-start.2
  460.0 3.6 copy-start.6
  460.0 4.0 copy-start.3
  460.0 9.1 %copy-start.4 = (bf16[1024,512]{1,0:T(8,128)(2,1)S(1)}, bf16[1024,512]{1,0:T(8,128)(2,1)}, u32[]{:S(2)}) copy-start(bf16[1024,512]{1,0:T(8,128)(2,1)} %param.23) | copy-start | bytes 3145732
  466.2 9.7 %all-to-all-start.2 = ((bf16[32,1,40]{2,1,0:T(2,128)(2,1)}), bf16[32,1,40]{2,1,0:T(2,128)(2,1)S(1)}, u32[]{:S(2)}, u32[]{:S(2)}) async-start(bf16[32,1,40]{2,1,0:T(2,128)(2,1)} %convert_element_type.78), calls=%async_computation.2 | async-start | bytes 32768 | tf_op jit(solution)/shard_map/all_to_all | solution.py:121
  469.0 4.0 copy-start.5
  616.7 5.1 copy-start.1
Sparse Core Ops, SparseCore 0:
  465.6 70.6 all-gather.1
where the time goes:
time: 630 us; the launch traced here: 629 us
  blocking collectives  237 us (38%)
  waiting for transfers between devices  171 us (27%)
  matrix products  116 us (18%)
  local copies, waits for them, and re-layouts  62.6 us (10%)
  other arithmetic  20.3 us (3%)
  between operations  14.3 us (2%)
  starting transfers between devices  6.58 us (1%)
    all_to_all x1, blocking collectives, local(): lax.all_to_all(outgoing.reshape(experts, capacity, 2 * model_width), ('gr...  237 us
    all_to_all x1, waiting for transfers between devices, local(): lax.all_to_all(pair_grad.reshape(experts, capacity, model_width), ('group...  117 us
    dot_general x20, matrix products, dot_rt(): lax.dot_general(left, right, (((1,), (1,)), ((), ())), preferred_element_...  56.2 us
    all_gather x1, waiting for transfers between devices, local(): lax.all_gather(grad_hidden, 'inner', axis=0, tiled=True)  52.7 us
    dot_general x16, matrix products, dot_lt(): lax.dot_general(left, right, (((0,), (0,)), ((), ())), preferred_element_...  30 us
    gather x1, local copies, waits for them, and re-layouts, local(): outgoing = send_rows[owner_token]  20.2 us
    dot_general x8, matrix products, attend(): jnp.dot(grad_scores, key_part, preferred_element_type=jnp.float32)  15.3 us
  transfers between devices with their start and end apart: 3, of which 3 were waited for; matrix products, arithmetic and copies ran while one was open for 2% of the time, Pallas kernels for 0%

commit v1 on v0

--- a/solution.py
+++ b/solution.py
@@ -138,9 +138,12 @@
     grad_hidden = (
         grad_out.astype(jnp.float32) + inv_rms * (scaled - normal_rows * inner_mean)
     ).astype(jnp.bfloat16)
-    grad_attn = dot_rt(lax.all_gather(grad_hidden, "inner", axis=0, tiled=True), out_proj).astype(
-        jnp.bfloat16
-    )
+    grad_attn = dot_rt(
+        jnp.concatenate(
+            lax.all_to_all(jnp.stack([grad_hidden] * lax.axis_size("inner")), "inner", 0, 0), axis=0
+        ),
+        out_proj,
+    ).astype(jnp.bfloat16)
     grad_items = by_head(grad_attn)
 
     def attend(block_item):

time: 630 us -> 655 us (1.040)
  waiting for transfers between devices: 171 us -> 198 us
  between operations: 14.3 us -> 1.19 us
    all_to_all x0 -> x1, waiting for transfers between devices: none -> 81.4 us  [local(): lax.all_to_all(jnp.stack([grad_hidden] * lax.axis_size('inner')), 'inner'...]
    all_gather x1 -> x0, waiting for transfers between devices: 52.7 us -> none  [local(): lax.all_gather(grad_hidden, 'inner', axis=0, tiled=True)]
  transfers between devices with their start and end apart: 3 -> 3, of which waited for: 3 -> 2; matrix products, arithmetic and copies ran while one was open for 2% -> 5% of each run, Pallas kernels for 0% -> 0%
where the time goes in v1:
time: 655 us; the launch traced here: 649 us
  blocking collectives  237 us (36%)
  waiting for transfers between devices  198 us (30%)
  matrix products  116 us (18%)
  local copies, waits for them, and re-layouts  64 us (10%)
  other arithmetic  19.5 us (3%)
  starting transfers between devices  12.5 us (2%)
    all_to_all x1, blocking collectives, local(): lax.all_to_all(outgoing.reshape(experts, capacity, 2 * model_width), ('gr...  237 us
    all_to_all x1, waiting for transfers between devices, local(): lax.all_to_all(pair_grad.reshape(experts, capacity, model_width), ('group...  117 us
    all_to_all x1, waiting for transfers between devices, local(): lax.all_to_all(jnp.stack([grad_hidden] * lax.axis_size('inner')), 'inner'...  81.4 us
    dot_general x20, matrix products, dot_rt(): lax.dot_general(left, right, (((1,), (1,)), ((), ())), preferred_element_...  56.4 us
    dot_general x16, matrix products, dot_lt(): lax.dot_general(left, right, (((0,), (0,)), ((), ())), preferred_element_...  30 us
    gather x1, local copies, waits for them, and re-layouts, local(): outgoing = send_rows[owner_token]  20.2 us
    dot_general x8, matrix products, attend(): jnp.dot(grad_scores, key_part, preferred_element_type=jnp.float32)  15.3 us
  transfers between devices with their start and end apart: 3, of which 2 were waited for; matrix products, arithmetic and copies ran while one was open for 5% of the time, Pallas kernels for 0%

profile of v1, /device:TPU:0, one launch (start us, length us, event | category | flops | bytes accessed | tf_op | source)
XLA Modules:
  0.0 649.2 jit_solution(4630642554560594967)
XLA Ops:
  2.5 9.0 %reduce-window.6 = s32[32,8,128]{2,1,0:T(8,128)S(1)} reduce-window(s32[32,8,128]{2,1,0:T(8,128)S(1)} %fusion.68, s32[]{:T(128)} %copy.83), window={size=1x1x128 pad=0_0x0_0x127_0}, to_apply=%region_1.0 | reduce-window | flops 4161536 | bytes 262148 | tf_op jit(solution)/shard_map/reduce-window
  12.2 4.3 scatter_custom_fusion
  19.0 2.2 fusion.56
  21.2 20.2 %gather_fusion = bf16[1280,4096]{1,0:T(8,128)(2,1)} fusion(bf16[129,4096]{1,0:T(8,128)(2,1)} %fusion.56, s32[2048]{0:T(1024)S(1)} %pad_clamp_fusion), kind=kCustom, calls=%fused_computation | custom fusion | bytes 20976640 | tf_op jit(solution)/shard_map/gather | solution.py:103
  41.4 237.5 %all_to_all.21 = bf16[32,40,4096]{2,1,0:T(8,128)(2,1)S(1)} all-to-all(bf16[32,40,4096]{2,1,0:T(8,128)(2,1)} %bitcast.147), channel_id=1, replica_groups=mesh['group'=4,'inner'=8] {'group','inner'}, dimensions={0} | all-to-all | bytes 20971520 | tf_op jit(solution)/shard_map/all_to_all | solution.py:104
  278.9 4.7 fusion.37
  283.6 6.4 fusion.39
  290.0 7.7 %multiply_reduce_fusion.1 = (bf16[1280]{0:T(1024)(128)(2,1)S(1)}, f32[1280,768]{0,1:T(8,128)}) fusion(f32[1280,768]{0,1:T(8,128)} %fusion.39, f32[1280,768]{0,1:T(8,128)S(1)} %fusion.37, bf16[1,768,2048]{2,1,0:T(8,128)(2,1)S(1)} %copy-done.10, bf16[1280,4096]{1,0:T(8,128)(2,1)S(1)} %bitcast.150), kind=kOutput, calls=%fused_computation.54 | convolution fusion | flops 4033411840 | bytes 20187648 | tf_op jit(solution)/shard_map/dot_general | solution.py:11
  297.7 12.7 %fusion.44 = f32[1280,2048]{1,0:T(8,128)} fusion(bf16[1,2048,768]{2,1,0:T(8,128)(2,1)S(1)} %copy-done, f32[1280,768]{0,1:T(8,128)S(1)} %fusion.37, f32[1280,768]{0,1:T(8,128)} %get-tuple-element.106, f32[1280,768]{0,1:T(8,128)} %fusion.39), kind=kOutput, calls=%fused_computation.59 | convolution fusion | flops 4036362240 | bytes 25427968 | tf_op jit(solution)/shard_map/dot_general | solution.py:11
  310.4 10.3 %add_convert_fusion = bf16[1280,2048]{1,0:T(8,128)(2,1)} fusion(f32[1280,2048]{1,0:T(8,128)} %fusion.44, bf16[1,2048,768]{2,1,0:T(8,128)(2,1)S(1)} %copy-done.11, f32[1280,768]{0,1:T(8,128)} %get-tuple-element.106, f32[1280,768]{0,1:T(8,128)S(1)} %fusion.37), kind=kOutput, calls=%fused_computation.45 | convolution fusion | flops 4037672960 | bytes 26738688 | tf_op jit(solution)/shard_map/dot_general | solution.py:11
  320.7 3.7 all-to-all-start.1
  325.3 116.6 %all-to-all-done.1 = bf16[32,40,2048]{2,1,0:T(8,128)(2,1)} async-done(((bf16[32,40,2048]{2,1,0:T(8,128)(2,1)}), bf16[32,40,2048]{2,1,0:T(8,128)(2,1)}, u32[]{:S(2)}, u32[]{:S(2)}) %all-to-all-start.1) | async-done | bytes 5242912 | tf_op jit(solution)/shard_map/all_to_all | solution.py:114
  442.0 2.5 all-to-all-start.2
  444.5 12.1 %gather_fusion.1 = bf16[1024,2048]{1,0:T(8,128)(2,1)} fusion(bf16[1280,2048]{1,0:T(8,128)(2,1)} %bitcast.10, s32[1024]{0:T(1024)S(1)} %broadcast_clamp_fusion), kind=kCustom, calls=%fused_computation.1 | custom fusion | bytes 8392704 | tf_op jit(solution)/shard_map/gather | solution.py:129
  456.6 3.5 fusion.41
  461.2 2.5 stack.2
  463.7 6.2 all-to-all-start.3
  474.5 6.8 %gather_fusion.2 = bf16[1024]{0:T(1024)(128)(2,1)S(1)} fusion(bf16[1280]{0:T(1024)(128)(2,1)S(1)} %reshape.162, s32[1024]{0:T(1024)S(1)} %broadcast_clamp_fusion), kind=kCustom, calls=%fused_computation.2 | custom fusion | bytes 8192 | tf_op jit(solution)/shard_map/gather | solution.py:130
  482.0 81.4 %all-to-all-done.3 = bf16[8,128,2048]{2,1,0:T(8,128)(2,1)} async-done(((bf16[8,128,2048]{2,1,0:T(8,128)(2,1)}), bf16[8,128,2048]{2,1,0:T(8,128)(2,1)}, u32[]{:S(2)}, u32[]{:S(2)}) %all-to-all-start.3) | async-done | bytes 4194336 | tf_op jit(solution)/shard_map/all_to_all | solution.py:143
  563.4 5.2 convolution_convert_fusion.1
  570.1 69.7 %while.15 = (s32[]{:T(128)}, bf16[8,512,128]{2,1,0:T(8,128)(2,1)}, bf16[8,512,128]{2,1,0:T(8,128)(2,1)}, bf16[8,512,128]{2,1,0:T(8,128)(2,1)}, bf16[8,512,128]{2...) while((s32[]{:T(128)}, bf16[8,512,128]{2,1,0:T(8,128)(2,1)}, ...), condition=%wide.region_11.12_spmd.clone, body=%wide.region_7.11_spmd.clone.sunk | while | flops 340589056 | bytes 10251357 | solution.py:166
  576.9 1.9 fusion.101
  585.6 1.9 fusion.101
  594.3 1.9 fusion.101
  603.0 1.9 fusion.101
  611.7 1.9 fusion.101
  620.4 1.9 fusion.101
  629.2 1.9 fusion.101
  637.9 1.9 fusion.101
  639.8 2.0 copy.48
  641.8 2.0 copy.49
  643.9 2.2 copy.47
  (117 shorter events, 70.7 us)
Async XLA Ops:
  0.6 278.2 %copy-start = (bf16[1,2048,768]{2,1,0:T(8,128)(2,1)S(1)}, bf16[1,2048,768]{2,1,0:T(8,128)(2,1)}, u32[]{:S(2)}) copy-start(bf16[1,2048,768]{2,1,0:T(8,128)(2,1)} %param.19) | copy-start | bytes 9437188
  278.9 4.7 copy-start.11
  283.6 6.4 copy-start.10
  320.7 3.7 copy-start.9
  320.7 121.2 %all-to-all-start.1 = ((bf16[32,40,2048]{2,1,0:T(8,128)(2,1)}), bf16[32,40,2048]{2,1,0:T(8,128)(2,1)}, u32[]{:S(2)}, u32[]{:S(2)}) async-start(bf16[32,40,2048]{2,1,0:T(8,128)(2,1)} %bitcast.151), calls=%async_computation.1 | async-start | bytes 10485760 | tf_op jit(solution)/shard_map/all_to_all | solution.py:114
  442.0 19.2 %all-to-all-start.2 = ((bf16[32,1,40]{2,1,0:T(2,128)(2,1)}), bf16[32,1,40]{2,1,0:T(2,128)(2,1)S(1)}, u32[]{:S(2)}, u32[]{:S(2)}) async-start(bf16[32,1,40]{2,1,0:T(2,128)(2,1)} %convert_element_type.78), calls=%async_computation.2 | async-start | bytes 32768 | tf_op jit(solution)/shard_map/all_to_all | solution.py:121
  456.6 3.5 copy-start.2
  456.6 3.5 copy-start.8
  456.6 4.0 copy-start.4
  461.2 2.5 copy-start.3
  463.7 6.3 copy-start.5
  463.7 99.7 %all-to-all-start.3 = ((bf16[8,128,2048]{2,1,0:T(8,128)(2,1)}), bf16[8,128,2048]{2,1,0:T(8,128)(2,1)}, u32[]{:S(2)}, u32[]{:S(2)}) async-start(bf16[8,128,2048]{2,1,0:T(8,128)(2,1)} %stack.2), calls=%async_computation.3 | async-start | bytes 8388608 | tf_op jit(solution)/shard_map/all_to_all | solution.py:143
  469.9 1.6 copy-start.6
  470.3 2.6 copy-start.7
  643.9 5.1 copy-start.1
